TPU v7x, 32 devices: a whole 2x2x4 slice. The times are simulated.
32 devices in a mesh: dp: 4 (over x, core), enc: 8 (over z, y).
Axes of the slice: x: 2, y: 2, z: 4, core: 2. Of those that a mesh axis runs over, the one named last changes fastest.
Arguments:
- hidden_states: bfloat16 [2048, 4096], P('dp', 'enc'), as said below
- dec_gain: bfloat16 [4096], replicated, as said below
- nbr_tokens: bfloat16 [48, 128, 4096], P('dp', 'enc'), as said below
- enc_gain: bfloat16 [4096], replicated, as said below
- query_weight: bfloat16 [4096, 4096], P(None, 'enc'), may hold values from -0.09375 to 0.09375
- key_weight: bfloat16 [4096, 4096], P(None, 'enc'), may hold values from -0.09375 to 0.09375
- value_weight: bfloat16 [4096, 4096], P(None, 'enc'), may hold values from -0.09375 to 0.09375
- out_weight: bfloat16 [4096, 4096], P('enc'), may hold values from -0.09375 to 0.09375
- cite_owner: int32 [64, 1], P('dp'), may hold values from 0 to 3; in each aligned block of 16 rows (0 to 15, 16 to 31, ...) at most 8 rows name the same one
- cite_local: int32 [32, 2], P('dp'), may hold values from 0 to 11
Outputs:
- block_out: bfloat16 [2048, 4096], P(('dp', 'enc'))
Inputs may be any that keep to these rules, and one draw needn't show every extreme that they name: `cite_owner`: among the citations of one index of dp, no owner is named more than 8 times, a bound that some block reaches. `hidden_states`: token rows have widely differing magnitudes. `nbr_tokens`: token rows have widely differing magnitudes. `dec_gain`: Positive. `enc_gain`: Positive.
All inputs are finite; a program needn't handle non-finite values.
Results may differ from a plain program's by a relative error of at most 0.013.
The roundings to bfloat16 on the way count: a program that leaves them out, or rounds other values in their place, can miss the bound.
Values may be sent and summed in bfloat16 or wider, within the bound.
A program may use at most 128 MiB of HBM per device.

v0:
```python
import jax
import jax.numpy as jnp
from jax import lax
from jax.sharding import PartitionSpec as P

HD = 128
SPAN = 64
NL = 128
NBRS = 2


def normalize(rows, gain):
    values = rows.astype(jnp.float32)
    scale = lax.rsqrt(jnp.mean(values * values, axis=-1, keepdims=True) + 1e-05)
    return (values * scale * gain.astype(jnp.float32)).astype(jnp.bfloat16)


def per_device(
    hidden_states,
    dec_gain,
    nbr_tokens,
    enc_gain,
    query_weight,
    key_weight,
    value_weight,
    out_weight,
    cite_owner,
    cite_local,
):
    kv_weight = jnp.concatenate((key_weight, value_weight), axis=1)

    def encode_tile(tile):
        return jnp.dot(
            normalize(tile, enc_gain), kv_weight, preferred_element_type=jnp.float32
        ).astype(jnp.bfloat16)

    encoded = lax.map(encode_tile, lax.all_gather(nbr_tokens, "enc", axis=1, tiled=True))
    whole = lax.all_gather(hidden_states, "enc", axis=1, tiled=True)
    queries = jnp.dot(
        normalize(whole, dec_gain), query_weight, preferred_element_type=jnp.float32
    ).astype(jnp.bfloat16)
    tok_rows = whole.shape[0]
    width = queries.shape[1]
    heads_here = width // HD
    span_count = tok_rows // SPAN
    owners = cite_owner[:, 0]
    tile_local = cite_local.reshape(-1)
    tiles_dev = encoded.shape[0]
    tile_ids = owners * tiles_dev + tile_local
    empty = jnp.zeros((owners.shape[0],) + encoded.shape[1:], jnp.bfloat16)
    piece = lax.all_gather(encoded, "dp", axis=0, tiled=True)
    count = piece.shape[0]
    inside = (tile_ids >= 0) & (tile_ids < count)
    picked = jnp.take(piece, jnp.clip(tile_ids, 0, count - 1), axis=0)
    cited = jnp.where(inside[:, None, None], picked, empty)
    kv = cited.reshape(span_count, NBRS * NL, 2, heads_here, HD)
    query_blocks = queries.reshape(span_count, SPAN, heads_here, HD)
    scores = jnp.einsum(
        "cqhd,ckhd->chqk", query_blocks, kv[:, :, 0], preferred_element_type=jnp.float32
    ) * HD ** (-0.5)
    weights = jax.nn.softmax(scores, axis=-1).astype(jnp.bfloat16)
    context = jnp.einsum(
        "chqk,ckhd->cqhd", weights, kv[:, :, 1], preferred_element_type=jnp.float32
    )
    context = context.astype(jnp.bfloat16).reshape(tok_rows, width)
    return lax.psum_scatter(
        jnp.dot(context, out_weight, preferred_element_type=jnp.float32).astype(jnp.bfloat16),
        "enc",
        scatter_dimension=0,
        tiled=True,
    )


def solution(mesh):
    in_specs = (
        P("dp", "enc"),
        P(),
        P("dp", "enc", None),
        P(),
        P(None, "enc"),
        P(None, "enc"),
        P(None, "enc"),
        P("enc", None),
        P("dp", None),
        P("dp", None),
    )
    out_specs = P(("dp", "enc"), None)
    return jax.shard_map(
        per_device, mesh=mesh, in_specs=in_specs, out_specs=out_specs, check_vma=False
    )
```

profile of v0, /device:TPU:0, one launch (start us, length us, event | category | flops | bytes accessed | tf_op | source)
XLA Modules:
  0.0 485.8 jit_solution(11635320714324521103)
XLA Ops:
  6.5 0.0 all-gather.4.cloned.1.call-start
  6.5 0.7 all-gather.4.cloned.1.call-update
  7.3 0.0 all-gather.8.cloned.1.call-start
  7.3 0.7 all-gather.8.cloned.1.call-update
  8.0 0.0 all-gather.6.cloned.1.call-start
  8.1 0.0 copy-start.2
  8.1 7.8 %pad_maximum_fusion = bf16[4096,1024]{1,0:T(8,128)(2,1)} fusion(bf16[4096,512]{1,0:T(8,128)(2,1)} %param.18, bf16[4096,512]{1,0:T(8,128)(2,1)} %param.17), kind=kLoop, calls=%fused_computation.21 | loop fusion | flops 16777216 | bytes 16777216 | tf_op jit(solution)/shard_map/concatenate | solution.py:30
  15.9 172.5 %all-gather.4.cloned.1.call-done = bf16[12,128,4096]{2,1,0:T(8,128)(2,1)} async-done(((bf16[12,16,4096]{2,1,0:T(8,128)(2,1)}), bf16[12,128,4096]{2,1,0:T(8,128)(2,1)}) %all-gather.4.cloned.1.call-update) | async-done | bytes 12582928 | tf_op jit(solution)/shard_map/all_gather | solution.py:37
  188.4 0.0 copy-done.2
  188.4 0.0 copy-start.4
  188.4 87.9 %while.10 = (s32[]{:T(128)}, bf16[12,128,1024]{2,1,0:T(8,128)(2,1)}, bf16[12,128,4096]{2,1,0:T(8,128)(2,1)}, bf16[4096]{0:T(1024)(128)(2,1)S(1)}, bf16[4096,1024]{1,0:T(8,128)(2,1)}, /*index=5*/s32[]{:T(128)}) while((s32[]{:T(128)}, bf16[12,128,1024]{2,1,0:T(8,128)(2,1)}, bf16[12,128,4096]{2,1,0:T(8,128)(2,1)}, bf16[4096]{0:T(1024)(128)(2,1)S(1)}, ...), condition=%wide.region_2.3_spmd, body=%wide.region_0.2_spmd.sunk | while | flops 1077547136 | bytes 10792017 | solution.py:37
  188.4 1.5 fusion.51
  189.9 5.7 %fusion.52 = bf16[12,128,1024]{2,1,0:T(8,128)(2,1)} fusion(bf16[12,128,1024]{2,1,0:T(8,128)(2,1)} %get-tuple-element.85, s32[]{:T(128)S(6)} %copy.47, bf16[4096,1024]{1,0:T(8,128)(2,1)} %get-tuple-element.94, f32[4096]{0:T(1024)S(1)} %convert_element_type.86, f32[128]{0:T(128)S(1)} %add_rsqrt_fusion.3, bf16[12,128,4096]{2,1,0:T(8,128)(2,1)} %get-tuple-element.92), kind=kOutput, calls=%fused_computation.8.clone.1 | convolution fusion | flops 1075970048 | bytes 9717248 | tf_op jit(solution)/shard_map/while/body/eval_jaxpr/dot_general | solution.py:33
  195.7 1.6 fusion.51
  197.3 5.8 %fusion.52 = bf16[12,128,1024]{2,1,0:T(8,128)(2,1)} fusion(bf16[12,128,1024]{2,1,0:T(8,128)(2,1)} %get-tuple-element.85, s32[]{:T(128)S(6)} %copy.47, bf16[4096,1024]{1,0:T(8,128)(2,1)} %get-tuple-element.94, f32[4096]{0:T(1024)S(1)} %convert_element_type.86, f32[128]{0:T(128)S(1)} %add_rsqrt_fusion.3, bf16[12,128,4096]{2,1,0:T(8,128)(2,1)} %get-tuple-element.92), kind=kOutput, calls=%fused_computation.8.clone.1 | convolution fusion | flops 1075970048 | bytes 9717248 | tf_op jit(solution)/shard_map/while/body/eval_jaxpr/dot_general | solution.py:33
  203.1 1.5 fusion.51
  204.7 5.8 %fusion.52 = bf16[12,128,1024]{2,1,0:T(8,128)(2,1)} fusion(bf16[12,128,1024]{2,1,0:T(8,128)(2,1)} %get-tuple-element.85, s32[]{:T(128)S(6)} %copy.47, bf16[4096,1024]{1,0:T(8,128)(2,1)} %get-tuple-element.94, f32[4096]{0:T(1024)S(1)} %convert_element_type.86, f32[128]{0:T(128)S(1)} %add_rsqrt_fusion.3, bf16[12,128,4096]{2,1,0:T(8,128)(2,1)} %get-tuple-element.92), kind=kOutput, calls=%fused_computation.8.clone.1 | convolution fusion | flops 1075970048 | bytes 9717248 | tf_op jit(solution)/shard_map/while/body/eval_jaxpr/dot_general | solution.py:33
  210.5 1.5 fusion.51
  212.0 5.8 %fusion.52 = bf16[12,128,1024]{2,1,0:T(8,128)(2,1)} fusion(bf16[12,128,1024]{2,1,0:T(8,128)(2,1)} %get-tuple-element.85, s32[]{:T(128)S(6)} %copy.47, bf16[4096,1024]{1,0:T(8,128)(2,1)} %get-tuple-element.94, f32[4096]{0:T(1024)S(1)} %convert_element_type.86, f32[128]{0:T(128)S(1)} %add_rsqrt_fusion.3, bf16[12,128,4096]{2,1,0:T(8,128)(2,1)} %get-tuple-element.92), kind=kOutput, calls=%fused_computation.8.clone.1 | convolution fusion | flops 1075970048 | bytes 9717248 | tf_op jit(solution)/shard_map/while/body/eval_jaxpr/dot_general | solution.py:33
  217.8 1.5 fusion.51
  219.3 5.7 %fusion.52 = bf16[12,128,1024]{2,1,0:T(8,128)(2,1)} fusion(bf16[12,128,1024]{2,1,0:T(8,128)(2,1)} %get-tuple-element.85, s32[]{:T(128)S(6)} %copy.47, bf16[4096,1024]{1,0:T(8,128)(2,1)} %get-tuple-element.94, f32[4096]{0:T(1024)S(1)} %convert_element_type.86, f32[128]{0:T(128)S(1)} %add_rsqrt_fusion.3, bf16[12,128,4096]{2,1,0:T(8,128)(2,1)} %get-tuple-element.92), kind=kOutput, calls=%fused_computation.8.clone.1 | convolution fusion | flops 1075970048 | bytes 9717248 | tf_op jit(solution)/shard_map/while/body/eval_jaxpr/dot_general | solution.py:33
  225.1 1.6 fusion.51
  226.6 5.9 %fusion.52 = bf16[12,128,1024]{2,1,0:T(8,128)(2,1)} fusion(bf16[12,128,1024]{2,1,0:T(8,128)(2,1)} %get-tuple-element.85, s32[]{:T(128)S(6)} %copy.47, bf16[4096,1024]{1,0:T(8,128)(2,1)} %get-tuple-element.94, f32[4096]{0:T(1024)S(1)} %convert_element_type.86, f32[128]{0:T(128)S(1)} %add_rsqrt_fusion.3, bf16[12,128,4096]{2,1,0:T(8,128)(2,1)} %get-tuple-element.92), kind=kOutput, calls=%fused_computation.8.clone.1 | convolution fusion | flops 1075970048 | bytes 9717248 | tf_op jit(solution)/shard_map/while/body/eval_jaxpr/dot_general | solution.py:33
  232.5 1.5 fusion.51
  234.0 5.8 %fusion.52 = bf16[12,128,1024]{2,1,0:T(8,128)(2,1)} fusion(bf16[12,128,1024]{2,1,0:T(8,128)(2,1)} %get-tuple-element.85, s32[]{:T(128)S(6)} %copy.47, bf16[4096,1024]{1,0:T(8,128)(2,1)} %get-tuple-element.94, f32[4096]{0:T(1024)S(1)} %convert_element_type.86, f32[128]{0:T(128)S(1)} %add_rsqrt_fusion.3, bf16[12,128,4096]{2,1,0:T(8,128)(2,1)} %get-tuple-element.92), kind=kOutput, calls=%fused_computation.8.clone.1 | convolution fusion | flops 1075970048 | bytes 9717248 | tf_op jit(solution)/shard_map/while/body/eval_jaxpr/dot_general | solution.py:33
  239.8 1.5 fusion.51
  241.4 5.7 %fusion.52 = bf16[12,128,1024]{2,1,0:T(8,128)(2,1)} fusion(bf16[12,128,1024]{2,1,0:T(8,128)(2,1)} %get-tuple-element.85, s32[]{:T(128)S(6)} %copy.47, bf16[4096,1024]{1,0:T(8,128)(2,1)} %get-tuple-element.94, f32[4096]{0:T(1024)S(1)} %convert_element_type.86, f32[128]{0:T(128)S(1)} %add_rsqrt_fusion.3, bf16[12,128,4096]{2,1,0:T(8,128)(2,1)} %get-tuple-element.92), kind=kOutput, calls=%fused_computation.8.clone.1 | convolution fusion | flops 1075970048 | bytes 9717248 | tf_op jit(solution)/shard_map/while/body/eval_jaxpr/dot_general | solution.py:33
  247.1 1.5 fusion.51
  248.6 5.9 %fusion.52 = bf16[12,128,1024]{2,1,0:T(8,128)(2,1)} fusion(bf16[12,128,1024]{2,1,0:T(8,128)(2,1)} %get-tuple-element.85, s32[]{:T(128)S(6)} %copy.47, bf16[4096,1024]{1,0:T(8,128)(2,1)} %get-tuple-element.94, f32[4096]{0:T(1024)S(1)} %convert_element_type.86, f32[128]{0:T(128)S(1)} %add_rsqrt_fusion.3, bf16[12,128,4096]{2,1,0:T(8,128)(2,1)} %get-tuple-element.92), kind=kOutput, calls=%fused_computation.8.clone.1 | convolution fusion | flops 1075970048 | bytes 9717248 | tf_op jit(solution)/shard_map/while/body/eval_jaxpr/dot_general | solution.py:33
  254.5 1.5 fusion.51
  256.0 5.7 %fusion.52 = bf16[12,128,1024]{2,1,0:T(8,128)(2,1)} fusion(bf16[12,128,1024]{2,1,0:T(8,128)(2,1)} %get-tuple-element.85, s32[]{:T(128)S(6)} %copy.47, bf16[4096,1024]{1,0:T(8,128)(2,1)} %get-tuple-element.94, f32[4096]{0:T(1024)S(1)} %convert_element_type.86, f32[128]{0:T(128)S(1)} %add_rsqrt_fusion.3, bf16[12,128,4096]{2,1,0:T(8,128)(2,1)} %get-tuple-element.92), kind=kOutput, calls=%fused_computation.8.clone.1 | convolution fusion | flops 1075970048 | bytes 9717248 | tf_op jit(solution)/shard_map/while/body/eval_jaxpr/dot_general | solution.py:33
  261.8 1.5 fusion.51
  263.3 5.7 %fusion.52 = bf16[12,128,1024]{2,1,0:T(8,128)(2,1)} fusion(bf16[12,128,1024]{2,1,0:T(8,128)(2,1)} %get-tuple-element.85, s32[]{:T(128)S(6)} %copy.47, bf16[4096,1024]{1,0:T(8,128)(2,1)} %get-tuple-element.94, f32[4096]{0:T(1024)S(1)} %convert_element_type.86, f32[128]{0:T(128)S(1)} %add_rsqrt_fusion.3, bf16[12,128,4096]{2,1,0:T(8,128)(2,1)} %get-tuple-element.92), kind=kOutput, calls=%fused_computation.8.clone.1 | convolution fusion | flops 1075970048 | bytes 9717248 | tf_op jit(solution)/shard_map/while/body/eval_jaxpr/dot_general | solution.py:33
  269.0 1.5 fusion.51
  270.6 5.7 %fusion.52 = bf16[12,128,1024]{2,1,0:T(8,128)(2,1)} fusion(bf16[12,128,1024]{2,1,0:T(8,128)(2,1)} %get-tuple-element.85, s32[]{:T(128)S(6)} %copy.47, bf16[4096,1024]{1,0:T(8,128)(2,1)} %get-tuple-element.94, f32[4096]{0:T(1024)S(1)} %convert_element_type.86, f32[128]{0:T(128)S(1)} %add_rsqrt_fusion.3, bf16[12,128,4096]{2,1,0:T(8,128)(2,1)} %get-tuple-element.92), kind=kOutput, calls=%fused_computation.8.clone.1 | convolution fusion | flops 1075970048 | bytes 9717248 | tf_op jit(solution)/shard_map/while/body/eval_jaxpr/dot_general | solution.py:33
  276.3 0.0 all-gather.6.cloned.1.call-update
  276.3 0.2 reduce-scatter.2.cloned.1.call-start
  276.6 0.0 copy-done.4
  276.6 0.1 copy.24
  276.7 0.1 reshape.63
  276.7 0.0 copy-done.5
  276.8 0.1 broadcast_in_dim.48
  276.9 0.1 copy.27
  277.0 0.1 mul.57
  277.1 0.1 copy.25
  277.2 0.0 copy-done.3
  277.2 0.1 broadcast_bitcast_fusion
  277.3 3.2 fusion.12
  280.5 0.2 copy-done.1
  280.7 5.2 %fusion.24 = bf16[512,512]{1,0:T(8,128)(2,1)S(1)} fusion(bf16[4096,512]{1,0:T(8,128)(2,1)} %param.16, bf16[512,4096]{1,0:T(8,128)(2,1)S(1)} %copy-done.1, f32[4096]{0:T(1024)S(1)} %convert_element_type.44, f32[512]{0:T(512)S(1)} %add_rsqrt_fusion.1), kind=kOutput, calls=%fused_computation.37 | convolution fusion | flops 2156134400 | bytes 8931328 | tf_op jit(solution)/shard_map/dot_general | solution.py:39
  285.9 0.1 reshape.64
  286.0 71.1 %all-gather.6.cloned.1.call-done = bf16[48,128,1024]{2,1,0:T(8,128)(2,1)} async-done(((bf16[12,128,1024]{2,1,0:T(8,128)(2,1)}), bf16[48,128,1024]{2,1,0:T(8,128)(2,1)}) %all-gather.6.cloned.1.call-update) | async-done | bytes 12582928 | tf_op jit(solution)/shard_map/all_gather | solution.py:51
  357.1 7.3 %gather_fusion = bf16[16,128,1024]{2,1,0:T(8,128)(2,1)} fusion(bf16[48,128,1024]{2,1,0:T(8,128)(2,1)} %all-gather.6.cloned.1.call-done, s32[1024]{0:T(1024)S(1)} %pad_clamp_fusion), kind=kCustom, calls=%fused_computation | custom fusion | bytes 8388672 | tf_op jit(solution)/shard_map/jit(_take)/gather | solution.py:54
  364.5 7.7 %reshape.75 = bf16[8,256,2,4,128]{4,3,2,1,0:T(4,128)(2,1)} reshape(bf16[16,128,1024]{2,1,0:T(8,128)(2,1)} %gather_fusion) | data formatting | bytes 8388608 | tf_op jit(solution)/shard_map/jit(_take)/gather | solution.py:54
  372.2 2.9 fusion.17
  375.1 0.0 copy-start
  375.1 1.9 copy-done
  377.0 0.8 fusion.21
  377.9 0.8 fusion.41
  378.6 5.2 %fusion.27 = bf16[8,64,4,128]{3,1,2,0:T(8,128)(2,1)S(1)} fusion(bf16[8,256,2,4,128]{4,1,3,0,2:T(8,128)(2,1)} %copy-done, f32[8,4,64]{2,1,0:T(4,128)S(1)} %fusion.41, f32[8,4,64,256]{3,2,1,0:T(8,128)S(1)} %fusion.21), kind=kOutput, calls=%fused_computation.38 | convolution fusion | flops 136579328 | bytes 4726784 | tf_op jit(solution)/shard_map/chqk,ckhd->cqhd/dot_general | solution.py:62
  383.8 0.4 copy.31
  384.3 6.5 %convolution_convert_fusion.1 = bf16[512,4096]{1,0:T(8,128)(2,1)} fusion(bf16[512,4096]{1,0:T(8,128)(2,1)} %param.19, bf16[64,8,4,128]{3,2,1,0:T(4,128)(2,1)S(1)} %bitcast.44), kind=kOutput, calls=%fused_computation.22 | convolution fusion | flops 2149580800 | bytes 8912896 | tf_op jit(solution)/shard_map/dot_general | solution.py:67
  390.7 0.0 reduce-scatter.2.cloned.1.call-update
  390.8 88.5 %reduce-scatter.2.cloned.1.call-done = bf16[64,4096]{1,0:T(8,128)(2,1)} async-done(((bf16[512,4096]{1,0:T(8,128)(2,1)}), bf16[64,4096]{1,0:T(8,128)(2,1)}) %reduce-scatter.2.cloned.1.call-update) | async-done | bytes 524304 | tf_op jit(solution)/shard_map/reduce_scatter | solution.py:66
  (35 shorter events, 0.2 us)
Async XLA Ops:
  6.5 181.8 %all-gather.4.cloned.1.call-start = ((), (), s32[]{:S(2)}) async-start(), calls=%async_computation.1 | async-start | bytes 14155776 | tf_op jit(solution)/shard_map/all_gather | solution.py:37
  7.3 270.0 %all-gather.8.cloned.1.call-start = ((), (), s32[]{:S(2)}) async-start(), calls=%async_computation.3 | async-start | bytes 4718592 | tf_op jit(solution)/shard_map/all_gather | solution.py:38
  8.0 349.1 %all-gather.6.cloned.1.call-start = ((), (), s32[]{:S(2)}) async-start(), calls=%async_computation.2 | async-start | bytes 15728640 | tf_op jit(solution)/shard_map/all_gather | solution.py:51
  8.1 180.3 %copy-start.2 = (bf16[4096]{0:T(1024)(128)(2,1)S(1)}, bf16[4096]{0:T(1024)(128)(2,1)}, u32[]{:S(2)}) copy-start(bf16[4096]{0:T(1024)(128)(2,1)} %param.15) | copy-start | bytes 24580
  188.4 88.2 %copy-start.4 = (s32[8,2]{0,1:T(2,128)S(1)}, s32[8,2]{0,1:T(2,128)}, u32[]{:S(2)}) copy-start(s32[8,2]{0,1:T(2,128)} %param.21) | copy-start | bytes 196
  188.4 88.4 %copy-start.5 = (s32[16,1]{0,1:T(1,128)S(1)}, s32[16,1]{0,1:T(1,128)}, u32[]{:S(2)}) copy-start(s32[16,1]{0,1:T(1,128)} %param.20) | copy-start | bytes 196
  188.4 88.8 %copy-start.3 = (bf16[4096]{0:T(1024)(128)(2,1)S(1)}, bf16[4096]{0:T(1024)(128)(2,1)}, u32[]{:S(2)}) copy-start(bf16[4096]{0:T(1024)(128)(2,1)} %param.13) | copy-start | bytes 24580
  276.3 202.9 %reduce-scatter.2.cloned.1.call-start = ((), (), s32[]{:S(2)}) async-start(), calls=%async_computation.4 | async-start | bytes 4718592 | tf_op jit(solution)/shard_map/reduce_scatter | solution.py:66
  277.3 3.5 copy-start.1
  375.1 1.9 copy-start
Sparse Core Ops, SparseCore 0:
  9.5 178.8 all-gather.3
  190.4 72.8 all-gather.7
  276.5 80.6 all-gather.5
  390.9 88.3 reduce-scatter.1
where the time goes:
time: 487 us; the launch traced here: 486 us
  waiting for transfers between devices  333 us (68%)
  matrix products  87.1 us (18%)
  other arithmetic  33.3 us (7%)
  local copies, waits for them, and re-layouts  18.3 us (4%)
  between operations  13.2 us (3%)
    all_gather x1, waiting for transfers between devices, per_device(): lax.all_gather(nbr_tokens, 'enc', axis=1, tiled=True)  172 us
    reduce_scatter x1, waiting for transfers between devices, per_device(): lax.psum_scatter(jnp.dot(context, out_weight, preferred_element_type=jnp....  88.5 us
    all_gather x1, waiting for transfers between devices, per_device(): piece = lax.all_gather(encoded, 'dp', axis=0, tiled=True)  71.1 us
    dot_general x12, matrix products, encode_tile(): jnp.dot(normalize(tile, enc_gain), kv_weight, preferred_element_type=jnp....  69.4 us
    reduce_sum x13, other arithmetic, normalize(): scale = lax.rsqrt(jnp.mean(values * values, axis=-1, keepdims=True) + 1e-05)  21.6 us
    gather x2, local copies, waits for them, and re-layouts, per_device(): picked = jnp.take(piece, jnp.clip(tile_ids, 0, count - 1), axis=0)  15.1 us
  transfers between devices with their start and end apart: 4, of which 3 were waited for; matrix products, arithmetic and copies ran while one was open for 22% of the time, Pallas kernels for 0%

commit v1 on v0

--- a/solution.py
+++ b/solution.py
@@ -7,6 +7,28 @@
 SPAN = 64
 NL = 128
 NBRS = 2
+
+
+def _fill_body(w_in, dim_at):
+    left_arr = jax.lax.axis_size("dp")
+    u1, everything, field_out = (left_arr, jax.lax.axis_index("dp"), w_in.shape[dim_at])
+    cards = tuple(((num, (num + 1) % u1) for num in range(u1)))
+    by_rank = tuple(((num, (num - 1) % u1) for num in range(u1)))
+    b_now = jnp.zeros((*w_in.shape[:dim_at], u1 * field_out, *w_in.shape[dim_at + 1 :]), w_in.dtype)
+    b_now = lax.dynamic_update_slice_in_dim(b_now, w_in, everything * field_out, axis=dim_at)
+    spare = lower = w_in
+    block_now = u1 // 2
+    for jj in [*range(1, block_now + 1)]:
+        spare = jax.lax.ppermute(spare, "dp", cards)
+        b_now = lax.dynamic_update_slice_in_dim(
+            b_now, spare, (everything - jj) % u1 * field_out, axis=dim_at
+        )
+        if jj < u1 - block_now:
+            lower = jax.lax.ppermute(lower, "dp", by_rank)
+            b_now = lax.dynamic_update_slice_in_dim(
+                b_now, lower, (everything + jj) % u1 * field_out, axis=dim_at
+            )
+    return b_now
 
 
 def normalize(rows, gain):
@@ -48,7 +70,7 @@
     tiles_dev = encoded.shape[0]
     tile_ids = owners * tiles_dev + tile_local
     empty = jnp.zeros((owners.shape[0],) + encoded.shape[1:], jnp.bfloat16)
-    piece = lax.all_gather(encoded, "dp", axis=0, tiled=True)
+    piece = _fill_body(encoded, 0)
     count = piece.shape[0]
     inside = (tile_ids >= 0) & (tile_ids < count)
     picked = jnp.take(piece, jnp.clip(tile_ids, 0, count - 1), axis=0)

time: 487 us -> 515 us (1.057)
  local copies, waits for them, and re-layouts: 18.3 us -> 38.3 us
  waiting for transfers between devices: 333 us -> 340 us
    ppermute x0 -> x3, waiting for transfers between devices: none -> 77.8 us  [the longest x2 77.8 us: _fill_body(): spare = jax.lax.ppermute(spare, 'dp', cards)]
    all_gather x1 -> x0, waiting for transfers between devices: 71.1 us -> none  [per_device(): piece = lax.all_gather(encoded, 'dp', axis=0, tiled=True)]
    dynamic_update_slice x0 -> x4, local copies, waits for them, and re-layouts: none -> 12 us  [the longest x2 6.09 us: _fill_body(): lax.dynamic_update_slice_in_dim(b_now, spare, (everything - jj) % u1 * fi...]
    broadcast_in_dim x0 -> x1, local copies, waits for them, and re-layouts: none -> 6.18 us  [_fill_body(): jnp.zeros((*w_in.shape[:dim_at], u1 * field_out, *w_in.shape[dim_at + 1:]...]
  transfers between devices with their start and end apart: 4 -> 6, of which waited for: 3 -> 4; matrix products, arithmetic and copies ran while one was open for 22% -> 24% of each run, Pallas kernels for 0% -> 0%
where the time goes in v1:
time: 515 us; the launch traced here: 514 us
  waiting for transfers between devices  340 us (66%)
  matrix products  87.3 us (17%)
  local copies, waits for them, and re-layouts  38.3 us (7%)
  other arithmetic  33.4 us (6%)
  between operations  13.2 us (3%)
    all_gather x1, waiting for transfers between devices, per_device(): lax.all_gather(nbr_tokens, 'enc', axis=1, tiled=True)  172 us
    reduce_scatter x1, waiting for transfers between devices, per_device(): lax.psum_scatter(jnp.dot(context, out_weight, preferred_element_type=jnp....  87.9 us
    ppermute x2, waiting for transfers between devices, _fill_body(): spare = jax.lax.ppermute(spare, 'dp', cards)  77.8 us
    dot_general x12, matrix products, encode_tile(): jnp.dot(normalize(tile, enc_gain), kv_weight, preferred_element_type=jnp....  69.4 us
    reduce_sum x13, other arithmetic, normalize(): scale = lax.rsqrt(jnp.mean(values * values, axis=-1, keepdims=True) + 1e-05)  21.6 us
    gather x2, local copies, waits for them, and re-layouts, per_device(): picked = jnp.take(piece, jnp.clip(tile_ids, 0, count - 1), axis=0)  15.1 us
  transfers between devices with their start and end apart: 6, of which 4 were waited for; matrix products, arithmetic and copies ran while one was open for 24% of the time, Pallas kernels for 0%

profile of v1, /device:TPU:0, one launch (start us, length us, event | category | flops | bytes accessed | tf_op | source)
XLA Modules:
  0.0 514.0 jit_solution(15262113475918379012)
XLA Ops:
  6.5 0.7 all-gather.3.cloned.1.call-update
  7.3 0.0 all-gather.5.cloned.1.call-start
  7.3 0.7 all-gather.5.cloned.1.call-update
  8.0 0.0 reduce-scatter.2.cloned.1.call-start
  8.1 0.0 copy-start.4
  8.1 7.8 %pad_maximum_fusion = bf16[4096,1024]{1,0:T(8,128)(2,1)} fusion(bf16[4096,512]{1,0:T(8,128)(2,1)} %param.18, bf16[4096,512]{1,0:T(8,128)(2,1)} %param.17), kind=kLoop, calls=%fused_computation.21 | loop fusion | flops 16777216 | bytes 16777216 | tf_op jit(solution)/shard_map/concatenate | solution.py:52
  15.9 172.5 %all-gather.3.cloned.1.call-done = bf16[12,128,4096]{2,1,0:T(8,128)(2,1)} async-done(((bf16[12,16,4096]{2,1,0:T(8,128)(2,1)}), bf16[12,128,4096]{2,1,0:T(8,128)(2,1)}) %all-gather.3.cloned.1.call-update) | async-done | bytes 12582928 | tf_op jit(solution)/shard_map/all_gather | solution.py:59
  188.4 88.0 %while.10 = (s32[]{:T(128)}, bf16[12,128,1024]{2,1,0:T(8,128)(2,1)}, bf16[12,128,4096]{2,1,0:T(8,128)(2,1)}, bf16[4096]{0:T(1024)(128)(2,1)S(1)}, bf16[4096,1024]{1,0:T(8,128)(2,1)}, /*index=5*/s32[]{:T(128)}) while((s32[]{:T(128)}, bf16[12,128,1024]{2,1,0:T(8,128)(2,1)}, bf16[12,128,4096]{2,1,0:T(8,128)(2,1)}, bf16[4096]{0:T(1024)(128)(2,1)S(1)}, ...), condition=%wide.region_2.3_spmd, body=%wide.region_0.2_spmd.sunk | while | flops 1077547136 | bytes 10792009 | solution.py:59
  188.4 1.5 fusion.51
  190.0 5.7 %fusion.52 = bf16[12,128,1024]{2,1,0:T(8,128)(2,1)} fusion(bf16[12,128,1024]{2,1,0:T(8,128)(2,1)} %get-tuple-element.85, s32[]{:T(128)} %get-tuple-element.84, bf16[4096,1024]{1,0:T(8,128)(2,1)} %get-tuple-element.94, f32[4096]{0:T(1024)S(1)} %convert_element_type.86, f32[128]{0:T(128)S(1)} %add_rsqrt_fusion.3, ...), kind=kOutput, calls=%fused_computation.8.clone.1 | convolution fusion | flops 1075970048 | bytes 9717248 | tf_op jit(solution)/shard_map/while/body/eval_jaxpr/dot_general | solution.py:55
  195.7 1.6 fusion.51
  197.3 5.8 %fusion.52 = bf16[12,128,1024]{2,1,0:T(8,128)(2,1)} fusion(bf16[12,128,1024]{2,1,0:T(8,128)(2,1)} %get-tuple-element.85, s32[]{:T(128)} %get-tuple-element.84, bf16[4096,1024]{1,0:T(8,128)(2,1)} %get-tuple-element.94, f32[4096]{0:T(1024)S(1)} %convert_element_type.86, f32[128]{0:T(128)S(1)} %add_rsqrt_fusion.3, ...), kind=kOutput, calls=%fused_computation.8.clone.1 | convolution fusion | flops 1075970048 | bytes 9717248 | tf_op jit(solution)/shard_map/while/body/eval_jaxpr/dot_general | solution.py:55
  203.2 1.5 fusion.51
  204.7 5.8 %fusion.52 = bf16[12,128,1024]{2,1,0:T(8,128)(2,1)} fusion(bf16[12,128,1024]{2,1,0:T(8,128)(2,1)} %get-tuple-element.85, s32[]{:T(128)} %get-tuple-element.84, bf16[4096,1024]{1,0:T(8,128)(2,1)} %get-tuple-element.94, f32[4096]{0:T(1024)S(1)} %convert_element_type.86, f32[128]{0:T(128)S(1)} %add_rsqrt_fusion.3, ...), kind=kOutput, calls=%fused_computation.8.clone.1 | convolution fusion | flops 1075970048 | bytes 9717248 | tf_op jit(solution)/shard_map/while/body/eval_jaxpr/dot_general | solution.py:55
  210.5 1.5 fusion.51
  212.0 5.8 %fusion.52 = bf16[12,128,1024]{2,1,0:T(8,128)(2,1)} fusion(bf16[12,128,1024]{2,1,0:T(8,128)(2,1)} %get-tuple-element.85, s32[]{:T(128)} %get-tuple-element.84, bf16[4096,1024]{1,0:T(8,128)(2,1)} %get-tuple-element.94, f32[4096]{0:T(1024)S(1)} %convert_element_type.86, f32[128]{0:T(128)S(1)} %add_rsqrt_fusion.3, ...), kind=kOutput, calls=%fused_computation.8.clone.1 | convolution fusion | flops 1075970048 | bytes 9717248 | tf_op jit(solution)/shard_map/while/body/eval_jaxpr/dot_general | solution.py:55
  217.8 1.5 fusion.51
  219.4 5.7 %fusion.52 = bf16[12,128,1024]{2,1,0:T(8,128)(2,1)} fusion(bf16[12,128,1024]{2,1,0:T(8,128)(2,1)} %get-tuple-element.85, s32[]{:T(128)} %get-tuple-element.84, bf16[4096,1024]{1,0:T(8,128)(2,1)} %get-tuple-element.94, f32[4096]{0:T(1024)S(1)} %convert_element_type.86, f32[128]{0:T(128)S(1)} %add_rsqrt_fusion.3, ...), kind=kOutput, calls=%fused_computation.8.clone.1 | convolution fusion | flops 1075970048 | bytes 9717248 | tf_op jit(solution)/shard_map/while/body/eval_jaxpr/dot_general | solution.py:55
  225.1 1.6 fusion.51
  226.7 5.9 %fusion.52 = bf16[12,128,1024]{2,1,0:T(8,128)(2,1)} fusion(bf16[12,128,1024]{2,1,0:T(8,128)(2,1)} %get-tuple-element.85, s32[]{:T(128)} %get-tuple-element.84, bf16[4096,1024]{1,0:T(8,128)(2,1)} %get-tuple-element.94, f32[4096]{0:T(1024)S(1)} %convert_element_type.86, f32[128]{0:T(128)S(1)} %add_rsqrt_fusion.3, ...), kind=kOutput, calls=%fused_computation.8.clone.1 | convolution fusion | flops 1075970048 | bytes 9717248 | tf_op jit(solution)/shard_map/while/body/eval_jaxpr/dot_general | solution.py:55
  232.5 1.5 fusion.51
  234.1 5.8 %fusion.52 = bf16[12,128,1024]{2,1,0:T(8,128)(2,1)} fusion(bf16[12,128,1024]{2,1,0:T(8,128)(2,1)} %get-tuple-element.85, s32[]{:T(128)} %get-tuple-element.84, bf16[4096,1024]{1,0:T(8,128)(2,1)} %get-tuple-element.94, f32[4096]{0:T(1024)S(1)} %convert_element_type.86, f32[128]{0:T(128)S(1)} %add_rsqrt_fusion.3, ...), kind=kOutput, calls=%fused_computation.8.clone.1 | convolution fusion | flops 1075970048 | bytes 9717248 | tf_op jit(solution)/shard_map/while/body/eval_jaxpr/dot_general | solution.py:55
  239.9 1.5 fusion.51
  241.4 5.7 %fusion.52 = bf16[12,128,1024]{2,1,0:T(8,128)(2,1)} fusion(bf16[12,128,1024]{2,1,0:T(8,128)(2,1)} %get-tuple-element.85, s32[]{:T(128)} %get-tuple-element.84, bf16[4096,1024]{1,0:T(8,128)(2,1)} %get-tuple-element.94, f32[4096]{0:T(1024)S(1)} %convert_element_type.86, f32[128]{0:T(128)S(1)} %add_rsqrt_fusion.3, ...), kind=kOutput, calls=%fused_computation.8.clone.1 | convolution fusion | flops 1075970048 | bytes 9717248 | tf_op jit(solution)/shard_map/while/body/eval_jaxpr/dot_general | solution.py:55
  247.2 1.5 fusion.51
  248.7 5.9 %fusion.52 = bf16[12,128,1024]{2,1,0:T(8,128)(2,1)} fusion(bf16[12,128,1024]{2,1,0:T(8,128)(2,1)} %get-tuple-element.85, s32[]{:T(128)} %get-tuple-element.84, bf16[4096,1024]{1,0:T(8,128)(2,1)} %get-tuple-element.94, f32[4096]{0:T(1024)S(1)} %convert_element_type.86, f32[128]{0:T(128)S(1)} %add_rsqrt_fusion.3, ...), kind=kOutput, calls=%fused_computation.8.clone.1 | convolution fusion | flops 1075970048 | bytes 9717248 | tf_op jit(solution)/shard_map/while/body/eval_jaxpr/dot_general | solution.py:55
  254.6 1.5 fusion.51
  256.1 5.7 %fusion.52 = bf16[12,128,1024]{2,1,0:T(8,128)(2,1)} fusion(bf16[12,128,1024]{2,1,0:T(8,128)(2,1)} %get-tuple-element.85, s32[]{:T(128)} %get-tuple-element.84, bf16[4096,1024]{1,0:T(8,128)(2,1)} %get-tuple-element.94, f32[4096]{0:T(1024)S(1)} %convert_element_type.86, f32[128]{0:T(128)S(1)} %add_rsqrt_fusion.3, ...), kind=kOutput, calls=%fused_computation.8.clone.1 | convolution fusion | flops 1075970048 | bytes 9717248 | tf_op jit(solution)/shard_map/while/body/eval_jaxpr/dot_general | solution.py:55
  261.8 1.5 fusion.51
  263.4 5.7 %fusion.52 = bf16[12,128,1024]{2,1,0:T(8,128)(2,1)} fusion(bf16[12,128,1024]{2,1,0:T(8,128)(2,1)} %get-tuple-element.85, s32[]{:T(128)} %get-tuple-element.84, bf16[4096,1024]{1,0:T(8,128)(2,1)} %get-tuple-element.94, f32[4096]{0:T(1024)S(1)} %convert_element_type.86, f32[128]{0:T(128)S(1)} %add_rsqrt_fusion.3, ...), kind=kOutput, calls=%fused_computation.8.clone.1 | convolution fusion | flops 1075970048 | bytes 9717248 | tf_op jit(solution)/shard_map/while/body/eval_jaxpr/dot_general | solution.py:55
  269.1 1.5 fusion.51
  270.7 5.7 %fusion.52 = bf16[12,128,1024]{2,1,0:T(8,128)(2,1)} fusion(bf16[12,128,1024]{2,1,0:T(8,128)(2,1)} %get-tuple-element.85, s32[]{:T(128)} %get-tuple-element.84, bf16[4096,1024]{1,0:T(8,128)(2,1)} %get-tuple-element.94, f32[4096]{0:T(1024)S(1)} %convert_element_type.86, f32[128]{0:T(128)S(1)} %add_rsqrt_fusion.3, ...), kind=kOutput, calls=%fused_computation.8.clone.1 | convolution fusion | flops 1075970048 | bytes 9717248 | tf_op jit(solution)/shard_map/while/body/eval_jaxpr/dot_general | solution.py:55
  276.4 0.0 collective-permute-start
  276.4 1.7 collective-permute-start.1
  278.1 67.0 %collective-permute-done = bf16[12,128,1024]{2,1,0:T(8,128)(2,1)S(1)} collective-permute-done((bf16[12,128,1024]{2,1,0:T(8,128)(2,1)}, bf16[12,128,1024]{2,1,0:T(8,128)(2,1)S(1)}, u32[]{:S(2)}, u32[]{:S(2)}) %collective-permute-start) | collective-permute-done | bytes 3145760 | tf_op jit(solution)/shard_map/ppermute | solution.py:22
  345.2 0.3 collective-permute-start.2
  345.5 0.1 copy.23
  345.5 0.1 reshape.63
  345.7 0.1 broadcast_in_dim.51
  345.7 0.1 copy.26
  345.9 0.1 mul.69
  346.0 0.1 copy.24
  346.1 0.1 broadcast_bitcast_fusion
  346.2 3.2 fusion.12
  349.4 0.2 copy-done.1
  349.6 5.4 %fusion.24 = bf16[512,512]{1,0:T(8,128)(2,1)} fusion(bf16[4096,512]{1,0:T(8,128)(2,1)} %param.16, bf16[512,4096]{1,0:T(8,128)(2,1)S(1)} %copy-done.1, f32[4096]{0:T(1024)S(1)} %convert_element_type.44, f32[512]{0:T(512)S(1)} %add_rsqrt_fusion.1), kind=kOutput, calls=%fused_computation.37 | convolution fusion | flops 2156134400 | bytes 8931328 | tf_op jit(solution)/shard_map/dot_general | solution.py:61
  355.0 2.0 reshape.64
  356.9 6.2 %broadcast_in_dim.55 = bf16[48,128,1024]{2,1,0:T(8,128)(2,1)} broadcast(bf16[]{:T(256)} %constant.75.clone.1), dimensions={} | broadcast | bytes 12582914 | tf_op jit(solution)/shard_map/broadcast_in_dim | solution.py:17
  363.1 2.0 constant_dynamic-update-slice_fusion.3
  365.1 2.2 constant_dynamic-update-slice_fusion.2
  367.3 3.9 constant_dynamic-update-slice_fusion.1
  371.2 10.8 %collective-permute-done.2 = bf16[12,128,1024]{2,1,0:T(8,128)(2,1)} collective-permute-done((bf16[12,128,1024]{2,1,0:T(8,128)(2,1)S(1)}, bf16[12,128,1024]{2,1,0:T(8,128)(2,1)}, u32[]{:S(2)}, u32[]{:S(2)}) %collective-permute-start.2) | collective-permute-done | bytes 3145760 | tf_op jit(solution)/shard_map/ppermute | solution.py:22
  382.0 3.9 constant_dynamic-update-slice_fusion
  385.9 7.3 %gather_fusion = bf16[16,128,1024]{2,1,0:T(8,128)(2,1)} fusion(bf16[48,128,1024]{2,1,0:T(8,128)(2,1)} %constant_dynamic-update-slice_fusion, s32[1024]{0:T(1024)S(1)} %pad_clamp_fusion), kind=kCustom, calls=%fused_computation | custom fusion | bytes 8388672 | tf_op jit(solution)/shard_map/jit(_take)/gather | solution.py:76
  393.2 7.7 %reshape.75 = bf16[8,256,2,4,128]{4,3,2,1,0:T(4,128)(2,1)} reshape(bf16[16,128,1024]{2,1,0:T(8,128)(2,1)} %gather_fusion) | data formatting | bytes 8388608 | tf_op jit(solution)/shard_map/jit(_take)/gather | solution.py:76
  400.9 3.0 fusion.17
  403.9 1.9 copy-done
  405.8 0.8 fusion.21
  406.7 0.8 fusion.41
  407.4 5.2 %fusion.27 = bf16[8,64,4,128]{3,1,2,0:T(8,128)(2,1)S(1)} fusion(bf16[8,256,2,4,128]{4,1,3,0,2:T(8,128)(2,1)} %copy-done, f32[8,4,64]{2,1,0:T(4,128)S(1)} %fusion.41, f32[8,4,64,256]{3,2,1,0:T(8,128)S(1)} %fusion.21), kind=kOutput, calls=%fused_computation.38 | convolution fusion | flops 136579328 | bytes 4726784 | tf_op jit(solution)/shard_map/chqk,ckhd->cqhd/dot_general | solution.py:84
  412.6 0.4 copy.30
  413.1 6.5 %convolution_convert_fusion.1 = bf16[512,4096]{1,0:T(8,128)(2,1)} fusion(bf16[512,4096]{1,0:T(8,128)(2,1)} %param.19, bf16[64,8,4,128]{3,2,1,0:T(4,128)(2,1)S(1)} %bitcast.44), kind=kOutput, calls=%fused_computation.22 | convolution fusion | flops 2149580800 | bytes 8912896 | tf_op jit(solution)/shard_map/dot_general | solution.py:89
  419.5 0.0 reduce-scatter.2.cloned.1.call-update
  419.6 87.9 %reduce-scatter.2.cloned.1.call-done = bf16[64,4096]{1,0:T(8,128)(2,1)} async-done(((bf16[512,4096]{1,0:T(8,128)(2,1)}), bf16[64,4096]{1,0:T(8,128)(2,1)}) %reduce-scatter.2.cloned.1.call-update) | async-done | bytes 524304 | tf_op jit(solution)/shard_map/reduce_scatter | solution.py:88
  (47 shorter events, 0.2 us)
Async XLA Ops:
  6.5 181.8 %all-gather.3.cloned.1.call-start = ((), (), s32[]{:S(2)}) async-start(), calls=%async_computation.1 | async-start | bytes 14155776 | tf_op jit(solution)/shard_map/all_gather | solution.py:59
  7.3 338.9 %all-gather.5.cloned.1.call-start = ((), (), s32[]{:S(2)}) async-start(), calls=%async_computation.2 | async-start | bytes 4718592 | tf_op jit(solution)/shard_map/all_gather | solution.py:60
  8.0 499.4 %reduce-scatter.2.cloned.1.call-start = ((), (), s32[]{:S(2)}) async-start(), calls=%async_computation.3 | async-start | bytes 4718592 | tf_op jit(solution)/shard_map/reduce_scatter | solution.py:88
  8.1 180.3 %copy-start.4 = (bf16[4096]{0:T(1024)(128)(2,1)S(1)}, bf16[4096]{0:T(1024)(128)(2,1)}, u32[]{:S(2)}) copy-start(bf16[4096]{0:T(1024)(128)(2,1)} %param.15) | copy-start | bytes 24580
  188.4 157.1 %copy-start.6 = (s32[8,2]{0,1:T(2,128)S(1)}, s32[8,2]{0,1:T(2,128)}, u32[]{:S(2)}) copy-start(s32[8,2]{0,1:T(2,128)} %param.21) | copy-start | bytes 196
  188.4 157.3 %copy-start.7 = (s32[16,1]{0,1:T(1,128)S(1)}, s32[16,1]{0,1:T(1,128)}, u32[]{:S(2)}) copy-start(s32[16,1]{0,1:T(1,128)} %param.20) | copy-start | bytes 196
  188.4 157.7 %copy-start.5 = (bf16[4096]{0:T(1024)(128)(2,1)S(1)}, bf16[4096]{0:T(1024)(128)(2,1)}, u32[]{:S(2)}) copy-start(bf16[4096]{0:T(1024)(128)(2,1)} %param.13) | copy-start | bytes 24580
  276.4 68.8 %collective-permute-start = (bf16[12,128,1024]{2,1,0:T(8,128)(2,1)}, bf16[12,128,1024]{2,1,0:T(8,128)(2,1)S(1)}, u32[]{:S(2)}, u32[]{:S(2)}) collective-permute-start(bf16[12,128,1024]{2,1,0:T(8,128)(2,1)} %get-tuple-element.32), channel_id=1, source_target_pairs={{0,8},{8,16},{16,24},{24,0},{1,9},{9,17},{17,25},{25,1},{2,10},{10... | collective-permute-start | bytes 9437192 | tf_op jit(solution)/shard_map/ppermute | solution.py:22
  276.4 90.9 %collective-permute-start.1 = (bf16[12,128,1024]{2,1,0:T(8,128)(2,1)}, bf16[12,128,1024]{2,1,0:T(8,128)(2,1)}, u32[]{:S(2)}, u32[]{:S(2)}) collective-permute-start(bf16[12,128,1024]{2,1,0:T(8,128)(2,1)} %get-tuple-element.32), channel_id=1, source_target_pairs={{0,24},{8,0},{16,8},{24,16},{1,25},{9,1},{17,9},{25,17},{2,26},{10... | collective-permute-start | bytes 9437192 | tf_op jit(solution)/shard_map/ppermute | solution.py:27
  345.2 36.8 %collective-permute-start.2 = (bf16[12,128,1024]{2,1,0:T(8,128)(2,1)S(1)}, bf16[12,128,1024]{2,1,0:T(8,128)(2,1)}, u32[]{:S(2)}, u32[]{:S(2)}) collective-permute-start(bf16[12,128,1024]{2,1,0:T(8,128)(2,1)S(1)} %collective-permute-done), channel_id=1, source_target_pairs={{0,8},{8,16},{16,24},{24,0},{1,9},{9,17},{17,25},{25,1},{2,10},{10... | collective-permute-start | bytes 9437192 | tf_op jit(solution)/shard_map/ppermute | solution.py:22
  346.2 3.5 copy-start.1
  356.9 6.2 %copy-start.2 = (bf16[12,128,1024]{2,1,0:T(8,128)(2,1)S(1)}, bf16[12,128,1024]{2,1,0:T(8,128)(2,1)}, u32[]{:S(2)}) copy-start(bf16[12,128,1024]{2,1,0:T(8,128)(2,1)} %get-tuple-element.32) | copy-start | bytes 9437188
  400.9 4.9 copy-start.3
  403.9 1.9 copy-start
Sparse Core Ops, SparseCore 0:
  9.5 178.8 all-gather.2
  190.4 72.8 all-gather.4
  419.7 87.7 reduce-scatter.1
